TPU v7x, 32 devices: a whole 2x2x4 slice. The times are simulated.
32 devices in a mesh: row: 8 (over z, y), col: 4 (over x, core).
Axes of the slice: x: 2, y: 2, z: 4, core: 2. Of those that a mesh axis runs over, the one named last changes fastest.
Arguments:
- ancestor: float32 [1024, 1024], P('row', 'col'), may hold values from -0.1875 to 0.1875
- factor: float32 [1024, 16, 128], P(('row', 'col')), may hold values from -1.5 to 1.5
- diag_inv: float32 [16, 128, 128], replicated, may hold values from -6 to 6
- structure: int32 [16, 96], replicated, may hold values from 0 to 127, as said below
Outputs:
- inverse_panel: float32 [1024, 16, 128], P(('row', 'col'))
- inverse_diagonal: float32 [16, 128, 128], replicated
Inputs may be any that keep to these rules, and one draw needn't show every extreme that they name: Each row of structure lists 96 different block numbers, in no particular order.
All inputs are finite; a program needn't handle non-finite values.
Results may differ from a plain program's by a relative error of at most 0.00007.
Values sent between devices are 32-bit elements; how exact they have to be, the bound alone decides.
A program may use at most 64 MiB of HBM per device.

v0:
```python
import jax
import jax.numpy as jnp
from jax import lax
from jax.sharding import PartitionSpec as P

RB = 8


def per_device(ancestor, factor, diag_inv, structure):
    row_devices = lax.axis_size("row")
    col_devices = lax.axis_size("col")
    ratio = row_devices // col_devices
    local_rows = factor.shape[0]
    width = factor.shape[2]
    first_row = (lax.axis_index("row") * col_devices + lax.axis_index("col")) * local_rows
    block_ids = (first_row + jnp.arange(local_rows, dtype=jnp.int32)) // RB
    matches = block_ids[:, None, None] == structure[None, :, :]
    row_mask = jnp.any(matches, axis=2).astype(jnp.float32)
    masked = factor * row_mask[:, :, None]
    count_sib = masked.shape[1]
    spread = masked.reshape(local_rows, count_sib * width)
    strided = lax.all_gather(spread, "row", axis=0, tiled=True)
    grouped = strided.reshape(col_devices, ratio, local_rows, count_sib * width)
    swapped = lax.all_to_all(grouped, "col", split_axis=0, concat_axis=0, tiled=True)
    columns = jnp.transpose(swapped, (1, 0, 2, 3)).reshape(
        ratio * col_devices * local_rows, count_sib * width
    )
    summed = lax.psum_scatter(
        jnp.dot(
            ancestor, columns, precision=lax.Precision.HIGHEST, preferred_element_type=jnp.float32
        ),
        "col",
        scatter_dimension=0,
        tiled=True,
    )
    panel = -summed.reshape(local_rows, count_sib, width)
    panel = panel * row_mask[:, :, None]
    local_update = jnp.einsum("bsw,bsv->swv", masked, panel, precision=lax.Precision.HIGHEST)
    total_update = lax.psum(local_update, ("row", "col"))
    return (panel, diag_inv - total_update)


def solution(mesh):
    placed = (P("row", "col"), P(("row", "col"), None, None), P(), P())
    return jax.shard_map(
        per_device,
        mesh=mesh,
        in_specs=placed,
        out_specs=(P(("row", "col"), None, None), P()),
        check_vma=False,
    )
```

profile of v0, /device:TPU:0, one launch (start us, length us, event | category | flops | bytes accessed | tf_op | source)
XLA Modules:
  0.0 264.8 jit_solution(8581905215952985030)
XLA Ops:
  7.2 0.0 copy-start
  7.2 0.0 all-gather.2.cloned.1.call-start
  7.2 1.4 compare_reduce_fusion
  8.7 1.1 broadcast_multiply_fusion.1
  9.7 0.8 copy.32
  10.5 0.0 all-gather.2.cloned.1.call-update
  10.6 0.0 reduce-scatter.4.cloned.1.call-start
  10.6 51.9 %all-gather.2.cloned.1.call-done = f32[256,2048]{1,0:T(8,128)} async-done(((f32[32,2048]{1,0:T(8,128)}), f32[256,2048]{1,0:T(8,128)}) %all-gather.2.cloned.1.call-update) | async-done | bytes 2097168 | tf_op jit(solution)/shard_map/all_gather | solution.py:22
  62.5 29.2 %all_to_all.5 = f32[4,2,32,2048]{3,2,1,0:T(8,128)S(1)} all-to-all(f32[4,2,32,2048]{3,2,1,0:T(8,128)} %bitcast.17), channel_id=1, replica_groups=mesh['row'=8,'col'=4] {'col'}, dimensions={0} | all-to-all | bytes 4194304 | tf_op jit(solution)/shard_map/all_to_all | solution.py:24
  91.8 0.2 copy.20
  92.0 0.0 copy-done
  92.0 3.6 %convolution_bitcast_fusion = f32[128,2048]{0,1:T(8,128)S(1)} fusion(f32[256,2048]{1,0:T(8,128)S(1)} %bitcast.14, f32[128,256]{1,0:T(8,128)S(1)} %copy-done), kind=kOutput, calls=%fused_computation | convolution fusion | flops 805306368 | bytes 3276800 | tf_op jit(solution)/shard_map/dot_general | solution.py:29
  95.6 1.3 copy.24
  96.9 0.0 reduce-scatter.4.cloned.1.call-update
  96.9 0.0 all-reduce.2.cloned.1.call-start
  97.0 22.5 %reduce-scatter.4.cloned.1.call-done = f32[32,2048]{1,0:T(8,128)} async-done(((f32[128,2048]{1,0:T(8,128)}), f32[32,2048]{1,0:T(8,128)}) %reduce-scatter.4.cloned.1.call-update) | async-done | bytes 262160
  119.5 1.3 copy.25
  120.8 0.1 neg.6
  120.9 0.0 copy-start.1
  120.9 0.3 copy.21
  121.2 0.1 broadcast_multiply_fusion
  121.3 0.0 copy-start.2
  121.4 2.8 %fusion = f32[16,128,128]{2,1,0:T(8,128)} fusion(f32[32,16,128]{2,1,0:T(8,128)S(1)} %broadcast_multiply_fusion, f32[32,16,128]{2,1,0:T(8,128)S(1)} %broadcast_multiply_fusion.1), kind=kOutput, calls=%fused_computation.2 | convolution fusion | flops 100663296 | bytes 1572864 | tf_op jit(solution)/shard_map/bsw,bsv->swv/dot_general | solution.py:38
  124.1 0.0 all-reduce.2.cloned.1.call-update
  124.2 131.8 %all-reduce.2.cloned.1.call-done = f32[16,128,128]{2,1,0:T(8,128)} async-done(((f32[16,128,128]{2,1,0:T(8,128)}), f32[16,128,128]{2,1,0:T(8,128)}) %all-reduce.2.cloned.1.call-update) | async-done | bytes 1048592 | tf_op jit(solution)/shard_map/psum | solution.py:39
  256.0 0.0 copy-done.1
  256.0 2.3 sub.10
  258.3 0.0 copy-done.2
  (2 shorter events, 0.0 us)
Async XLA Ops:
  7.2 84.8 %copy-start = (f32[128,256]{1,0:T(8,128)S(1)}, f32[128,256]{1,0:T(8,128)}, u32[]{:S(2)}) copy-start(f32[128,256]{1,0:T(8,128)} %param.4) | copy-start | bytes 393220
  7.2 55.3 %all-gather.2.cloned.1.call-start = ((), (), s32[]{:S(2)}) async-start(), calls=%async_computation.2 | async-start | bytes 2359296 | tf_op jit(solution)/shard_map/all_gather | solution.py:22
  10.6 108.9 %reduce-scatter.4.cloned.1.call-start = ((), (), s32[]{:S(2)}) async-start(), calls=%async_computation.4 | async-start | bytes 1310720
  96.9 159.1 %all-reduce.2.cloned.1.call-start = ((), (), s32[]{:S(2)}) async-start(), calls=%async_computation.3 | async-start | bytes 2097152 | tf_op jit(solution)/shard_map/psum | solution.py:39
  120.9 135.1 %copy-start.1 = (f32[16,128,128]{2,1,0:T(8,128)S(1)}, f32[16,128,128]{2,1,0:T(8,128)}, u32[]{:S(2)}) copy-start(f32[16,128,128]{2,1,0:T(8,128)} %param.6) | copy-start | bytes 3145732
  121.3 137.0 %copy-start.2 = (f32[32,16,128]{2,1,0:T(8,128)}, f32[32,16,128]{2,1,0:T(8,128)S(1)}, u32[]{:S(2)}) copy-start(f32[32,16,128]{2,1,0:T(8,128)S(1)} %broadcast_multiply_fusion) | copy-start | bytes 786436
Sparse Core Ops, SparseCore 0:
  10.7 51.7 all-gather.1
  97.1 22.3 reduce-scatter.3
  125.3 130.6 all-reduce.1
where the time goes:
time: 265 us
  waiting for transfers between devices  206 us (78%)
  blocking collectives  29.2 us (11%)
  between operations  13.9 us (5%)
  matrix products  6.38 us (2%)
  other arithmetic  4.99 us (2%)
  local copies, waits for them, and re-layouts  3.94 us (1%)
    psum x1, waiting for transfers between devices, per_device(): total_update = lax.psum(local_update, ('row', 'col'))  132 us
    all_gather x1, waiting for transfers between devices, per_device(): strided = lax.all_gather(spread, 'row', axis=0, tiled=True)  51.9 us
    all_to_all x1, blocking collectives, per_device(): lax.all_to_all(grouped, 'col', split_axis=0, concat_axis=0, tiled=True)  29.2 us
    unnamed x4, waiting for transfers between devices  22.6 us
  transfers between devices with their start and end apart: 3, of which 3 were waited for; matrix products, arithmetic and copies ran while one was open for 0% of the time, Pallas kernels for 0%

commit v1 on v0

v1 whole, which is shorter than its diff:
```python
import functools

import jax
import jax.numpy as jnp
from jax import lax
from jax.experimental import pallas as pl
from jax.experimental.pallas import tpu as pltpu
from jax.sharding import PartitionSpec as P

RB = 8
MESH = pl.DeviceIdType.MESH
HIGHEST = lax.Precision.HIGHEST


def kernel(
    line, group, lows, cols,
    a_ref, m_ref, c_out, u_out,
    a_full, b_buf, c_buf, u_part, u_recv,
    local_sem, a_send, a_recv, b_send, b_recv, z_send,
    c_send, c_recv, r_send, r_recv, l_send, u_send, u_recv_sem,
):
    row, col = lax.axis_index("row"), lax.axis_index("col")
    h, p = row // lows, (row % lows) * cols + col
    rows, width = m_ref.shape[1], m_ref.shape[2]
    slab = group * rows
    chunk = u_recv.shape[1]
    sib_width = u_part.shape[1]
    per = width // sib_width
    me = h * group + p

    def dev(hq, pq):
        return (hq * lows + pq // cols, pq % cols)

    def remote(src, dst, send, recv, target):
        return pltpu.make_async_remote_copy(
            src_ref=src, dst_ref=dst, send_sem=send, recv_sem=recv,
            device_id=target, device_id_type=MESH,
        )

    def peer(k, n, own):
        return lax.rem(own + k, n)

    def each_plane(body):
        def step(k, carry):
            body(k, peer(k, group, p))
            return carry
        lax.fori_loop(1, group, step, 0)

    def each_line(body):
        def step(k, carry):
            body(k, peer(k, line, h))
            return carry
        lax.fori_loop(1, line, step, 0)

    barrier = pltpu.get_barrier_semaphore()
    each_plane(lambda k, q: pl.semaphore_signal(
        barrier, inc=1, device_id=dev(h, q), device_id_type=MESH))
    each_line(lambda k, hq: pl.semaphore_signal(
        barrier, inc=1, device_id=dev(hq, p), device_id_type=MESH))
    pl.semaphore_wait(barrier, group + line - 2)

    def piece(hs, q):
        return b_buf.at[pl.ds(pl.multiple_of((hs * group + q) * rows, rows), rows)]

    def b_copy(k, q):
        return remote(m_ref.at[q], piece(h, p), b_send.at[k], b_recv.at[me], dev(h, q))

    def b_wait(hs, q):
        remote(piece(hs, q), piece(hs, q), b_send.at[0], b_recv.at[hs * group + q],
               dev(h, p)).wait_recv()

    def forward(hs, q, to_right):
        side = 0 if to_right else 1
        target = dev(h + 1, p) if to_right else dev(h - 1, p)
        remote(piece(hs, q), piece(hs, q), z_send.at[side, hs],
               b_recv.at[hs * group + q], target).start()

    def a_copy(k, q):
        return remote(a_ref, a_full.at[p], a_send.at[k], a_recv.at[p], dev(h, q))

    own_a = pltpu.make_async_copy(a_ref, a_full.at[p], local_sem.at[0])
    own_b = pltpu.make_async_copy(m_ref.at[p], piece(h, p), local_sem.at[1])
    own_b.start()
    each_plane(lambda k, q: b_copy(k, q).start())
    own_a.start()
    own_b.wait()

    def first(k, carry):
        q = lax.rem(p + group - k, group)

        @pl.when(k > 0)
        def _():
            b_wait(h, q)

        @pl.when(h + 1 < line)
        def _():
            forward(h, q, True)

        @pl.when(h > 0)
        def _():
            forward(h, q, False)

        @pl.when(k == 0)
        def _():
            each_plane(lambda j, r: a_copy(j, r).start())
        return carry

    lax.fori_loop(0, group, first, 0)

    def relay(t, carry):
        def one(k, inner):
            q = lax.rem(p + group - k, group)

            @pl.when(h >= t)
            def _():
                b_wait(h - t, q)

                @pl.when(h + 1 < line)
                def _():
                    forward(h - t, q, True)

            @pl.when(h + t < line)
            def _():
                b_wait(h + t, q)

                @pl.when(h > 0)
                def _():
                    forward(h + t, q, False)
            return inner
        lax.fori_loop(0, group, one, 0)
        return carry

    lax.fori_loop(1, line - 1, relay, 0)

    c_buf[...] = jnp.zeros_like(c_buf)
    own_a.wait()
    each_plane(lambda k, q: remote(
        a_full.at[q], a_full.at[q], a_send.at[0], a_recv.at[q], dev(h, p)).wait_recv())
    a_rows, depth = a_ref.shape
    step = min(slab, depth)

    def multiply(hs):
        for part in range(slab // step):
            start = hs * slab + part * step
            block = b_buf[pl.ds(pl.multiple_of(start, step), step), :]
            at, off = start // depth, start % depth
            for lo in range(lows):
                if step == depth:
                    left = a_full[lo * cols + at]
                else:
                    left = a_full[lo * cols + at, :, pl.ds(pl.multiple_of(off, step), step)]
                c_buf[lo * a_rows:(lo + 1) * a_rows, :] += jnp.dot(
                    left, block, precision=HIGHEST, preferred_element_type=jnp.float32
                )

    def arrived(hs, carry):
        @pl.when((hs - h < line - 1) & (h - hs < line - 1))
        def _():
            multiply(hs)
        return carry

    lax.fori_loop(0, line, arrived, 0)
    last = line - 1

    @pl.when((h == 0) | (h == last))
    def _():
        far = last - h

        def wait_far(k, carry):
            b_wait(far, lax.rem(p + group - k, group))
            return carry

        lax.fori_loop(0, group, wait_far, 0)
        multiply(far)

    mine = pl.ds(pl.multiple_of(h * slab, slab), slab)
    for s in range(per):
        lanes = slice(s * sib_width, (s + 1) * sib_width)
        u_part[s * sib_width:(s + 1) * sib_width, :] = lax.dot_general(
            b_buf[mine, lanes], c_buf[:, lanes], (((0,), (0,)), ((), ())),
            precision=HIGHEST, preferred_element_type=jnp.float32,
        )

    def r_copy(k, hq):
        return remote(u_part.at[pl.ds(pl.multiple_of(hq * chunk, chunk), chunk)],
                      u_recv.at[h], r_send.at[k], r_recv.at[h], dev(hq, p))

    def c_copy(k, q):
        return remote(c_buf.at[pl.ds(pl.multiple_of(q * rows, rows), rows)], c_out.at[p],
                      c_send.at[k], c_recv.at[p], dev(h, q))

    each_line(lambda k, hq: r_copy(k, hq).start())
    each_plane(lambda k, q: c_copy(k, q).start())
    c_out[p] = c_buf[pl.ds(pl.multiple_of(p * rows, rows), rows), :]
    u_recv[h] = u_part[pl.ds(pl.multiple_of(h * chunk, chunk), chunk), :]
    each_line(lambda k, hq: remote(
        u_recv.at[hq], u_recv.at[hq], r_send.at[0], r_recv.at[hq], dev(h, p)).wait_recv())
    total = u_recv[0]
    for hs in range(1, line):
        total = total + u_recv[hs]

    def u_at(hs, q):
        return pl.ds(pl.multiple_of((q * line + hs) * chunk, chunk), chunk)

    u_out[u_at(h, p), :] = total

    def l_copy(k, hq):
        here = u_out.at[u_at(h, p)]
        return remote(here, here, l_send.at[k], u_recv_sem.at[me], dev(hq, p))

    def u_copy(hs, k, q):
        here = u_out.at[u_at(hs, p)]
        return remote(here, here, u_send.at[hs, k], u_recv_sem.at[hs * group + p], dev(h, q))

    def u_wait(hs, q):
        here = u_out.at[u_at(hs, q)]
        remote(here, here, l_send.at[0], u_recv_sem.at[hs * group + q], dev(h, p)).wait_recv()

    each_line(lambda k, hq: l_copy(k, hq).start())
    each_plane(lambda k, q: u_copy(h, k, q).start())

    def spread(k, hq):
        u_wait(hq, p)
        each_plane(lambda j, q: u_copy(hq, j, q).start())

    each_line(spread)

    each_plane(lambda k, q: b_copy(k, q).wait_send())
    each_plane(lambda k, q: a_copy(k, q).wait_send())
    each_plane(lambda k, q: c_copy(k, q).wait_send())
    each_line(lambda k, hq: r_copy(k, hq).wait_send())
    each_line(lambda k, hq: l_copy(k, hq).wait_send())

    def drain(hs, carry):
        whole = b_buf.at[pl.ds(pl.multiple_of(hs * slab, slab), slab)]

        @pl.when((hs <= h) & (h + 1 < line))
        def _():
            remote(whole, whole, z_send.at[0, hs], b_recv.at[0], dev(h, p)).wait_send()

        @pl.when((hs >= h) & (h > 0))
        def _():
            remote(whole, whole, z_send.at[1, hs], b_recv.at[0], dev(h, p)).wait_send()

        each_plane(lambda k, q: u_copy(hs, k, q).wait_send())
        each_plane(lambda k, q: u_wait(hs, q))
        return carry

    lax.fori_loop(0, line, drain, 0)
    each_plane(lambda k, q: remote(
        c_out.at[q], c_out.at[q], c_send.at[0], c_recv.at[q], dev(h, p)).wait_recv())


def per_device(row_devices, col_devices, ancestor, factor, diag_inv, structure):
    local_rows, count_sib, width = factor.shape
    lows = max(1, min(row_devices, count_sib // (2 * col_devices)))
    line, group = row_devices // lows, lows * col_devices
    per = count_sib // group
    chunk = per * width // line
    first_row = (lax.axis_index("row") * col_devices + lax.axis_index("col")) * local_rows
    block_ids = (first_row + jnp.arange(local_rows, dtype=jnp.int32)) // RB
    matches = block_ids[:, None, None] == structure[None, :, :]
    row_mask = jnp.any(matches, axis=2).astype(jnp.float32)
    masked = factor * row_mask[:, :, None]
    sent = jnp.transpose(masked.reshape(local_rows, group, per * width), (1, 0, 2))
    dma = pltpu.SemaphoreType.DMA
    vmem = pl.BlockSpec(memory_space=pltpu.VMEM)
    f32 = jnp.float32
    product, update = pl.pallas_call(
        functools.partial(kernel, line, group, lows, col_devices),
        out_shape=(
            jax.ShapeDtypeStruct((group, local_rows, per * width), f32),
            jax.ShapeDtypeStruct((count_sib * width, width), f32),
        ),
        in_specs=[vmem, vmem],
        out_specs=(vmem, vmem),
        scratch_shapes=[
            pltpu.VMEM((group,) + ancestor.shape, f32),
            pltpu.VMEM((line * group * local_rows, per * width), f32),
            pltpu.VMEM((group * local_rows, per * width), f32),
            pltpu.VMEM((per * width, width), f32),
            pltpu.VMEM((line, chunk, width), f32),
            dma((2,)), dma((group,)), dma((group,)), dma((group,)), dma((line * group,)),
            dma((2, line)), dma((group,)), dma((group,)), dma((line,)), dma((line,)),
            dma((line,)), dma((line, group)), dma((line * group,)),
        ],
        compiler_params=pltpu.CompilerParams(collective_id=0, has_side_effects=True),
    )(ancestor, sent)
    product = jnp.transpose(product, (1, 0, 2)).reshape(local_rows, count_sib, width)
    panel = -product * row_mask[:, :, None]
    return panel, diag_inv + update.reshape(count_sib, width, width)


def solution(mesh):
    placed = (P("row", "col"), P(("row", "col"), None, None), P(), P())
    return jax.shard_map(
        functools.partial(per_device, mesh.shape["row"], mesh.shape["col"]),
        mesh=mesh,
        in_specs=placed,
        out_specs=(P(("row", "col"), None, None), P()),
        check_vma=False,
    )
```

time: 265 us -> 54.3 us (0.20)
  waiting for transfers between devices: 206 us -> 0 us
  Pallas kernels: 0 us -> 46.8 us
  blocking collectives: 29.2 us -> 0 us
  between operations: 13.9 us -> 0.71 us
  matrix products: 6.38 us -> 0 us
    psum x1 -> x0, waiting for transfers between devices: 132 us -> none  [per_device(): total_update = lax.psum(local_update, ('row', 'col'))]
    all_gather x1 -> x0, waiting for transfers between devices: 51.9 us -> none  [per_device(): strided = lax.all_gather(spread, 'row', axis=0, tiled=True)]
    pallas_call x0 -> x1, Pallas kernels: none -> 46.8 us  [per_device(): pl.pallas_call(functools.partial(kernel, line, group, lows, col_devices),...]
    all_to_all x1 -> x0, blocking collectives: 29.2 us -> none  [per_device(): lax.all_to_all(grouped, 'col', split_axis=0, concat_axis=0, tiled=True)]
    unnamed x4 -> x0, waiting for transfers between devices: 22.6 us -> none
    dot_general x2 -> x0, matrix products: 6.38 us -> none  [the longest x1 3.59 us: per_device(): jnp.dot(ancestor, columns, precision=lax.Precision.HIGHEST, preferred_ele...]
    unnamed x9 -> x6, local copies, waits for them, and re-layouts: 3.39 us -> 0.68 us
  transfers between devices with their start and end apart: 3 -> 0, of which waited for: 3 -> 0; matrix products, arithmetic and copies ran while one was open for 0% -> 0% of each run, Pallas kernels for 0% -> 0%
where the time goes in v1:
time: 54.3 us; the launch traced here: 54 us
  Pallas kernels  46.8 us (86%)
  other arithmetic  4.83 us (9%)
  local copies, waits for them, and re-layouts  1.72 us (3%)
  between operations  0.71 us (1%)
    pallas_call x1, Pallas kernels, per_device(): pl.pallas_call(functools.partial(kernel, line, group, lows, col_devices),...  46.8 us
    neg x1, other arithmetic, per_device(): panel = -product * row_mask[:, :, None]  1.12 us

profile of v1, /device:TPU:0, one launch (start us, length us, event | category | flops | bytes accessed | tf_op | source)
XLA Modules:
  0.0 54.0 jit_solution(15537842270007716947)
XLA Ops:
  0.6 0.0 copy-start.2
  0.7 0.7 %copy-done.2 = s32[16,96]{1,0:T(8,128)S(1)} copy-done((s32[16,96]{1,0:T(8,128)S(1)}, s32[16,96]{1,0:T(8,128)}, u32[]{:S(2)}) %copy-start.2) | copy-done | bytes 6168
  1.3 0.7 %compare_reduce_fusion = pred[32,16]{1,0:T(8,128)(4,1)S(1)} fusion(s32[16,96]{1,0:T(8,128)S(1)} %copy-done.2, s32[32]{0:T(128)S(1)} %and_select_fusion), kind=kLoop, calls=%fused_computation.2 | loop fusion | flops 97792 | bytes 6784 | tf_op jit(solution)/shard_map/reduce_or | solution.py:263
  2.0 1.1 %broadcast_multiply_fusion.1 = f32[32,16,128]{2,1,0:T(8,128)S(1)} fusion(f32[32,16,128]{2,1,0:T(8,128)} %param.5, f32[32,16]{1,0:T(8,128)S(1)} %convert_element_type.7), kind=kLoop, calls=%fused_computation.4 | loop fusion | flops 65536 | bytes 526336 | tf_op jit(solution)/shard_map/mul | solution.py:264
  3.1 0.1 reshape.35
  3.2 0.8 %copy.11 = f32[32,8,256]{2,0,1:T(8,128)} copy(f32[32,8,256]{2,1,0:T(8,128)S(1)} %reshape.35) | data formatting | bytes 524288 | tf_op jit(solution)/shard_map/reshape | solution.py:265
  4.0 46.8 %shard_map.59 = (f32[8,32,256]{2,1,0:T(8,128)}, f32[2048,128]{1,0:T(8,128)}) custom-call(f32[128,256]{1,0:T(8,128)} %a_ref.1, f32[8,32,256]{2,1,0:T(8,128)} %bitcast.7), custom_call_target="tpu_custom_call" | custom-call | tf_op jit(solution)/shard_map/pallas_call | solution.py:269
  50.8 0.0 copy-start
  50.8 0.0 copy-start.1
  50.8 1.1 %negate_bitcast_fusion = f32[32,8,256]{2,0,1:T(8,128)S(1)} fusion(f32[8,32,256]{2,1,0:T(8,128)} %get-tuple-element.4), kind=kLoop, calls=%fused_computation.1 | loop fusion | flops 65536 | bytes 524288 | tf_op jit(solution)/shard_map/neg | solution.py:290
  51.9 0.2 copy.9
  52.1 0.8 %broadcast_multiply_fusion = f32[32,16,128]{2,1,0:T(8,128)} fusion(f32[32,16,128]{2,1,0:T(8,128)S(1)} %neg.11, f32[32,16]{1,0:T(8,128)S(1)} %convert_element_type.7), kind=kLoop, calls=%fused_computation.3 | loop fusion | flops 65536 | bytes 526336 | tf_op jit(solution)/shard_map/mul | solution.py:290
  52.9 0.0 copy-done
  53.0 0.0 copy-done.1
  53.0 1.1 %add.24 = f32[16,128,128]{2,1,0:T(8,128)} add(f32[16,128,128]{2,1,0:T(8,128)S(1)} %copy-done, f32[16,128,128]{2,1,0:T(8,128)S(1)} %bitcast.6) | non-fusion elementwise | flops 262144 | bytes 3145728 | tf_op jit(solution)/shard_map/add | solution.py:291
  (3 shorter events, 0.0 us)
Async XLA Ops:
  0.6 0.7 %copy-start.2 = (s32[16,96]{1,0:T(8,128)S(1)}, s32[16,96]{1,0:T(8,128)}, u32[]{:S(2)}) copy-start(s32[16,96]{1,0:T(8,128)} %param.7) | copy-start | bytes 18436
  50.8 2.2 %copy-start = (f32[16,128,128]{2,1,0:T(8,128)S(1)}, f32[16,128,128]{2,1,0:T(8,128)}, u32[]{:S(2)}) copy-start(f32[16,128,128]{2,1,0:T(8,128)} %param.6) | copy-start | bytes 3145732
  50.8 2.2 %copy-start.1 = (f32[2048,128]{1,0:T(8,128)S(1)}, f32[2048,128]{1,0:T(8,128)}, u32[]{:S(2)}) copy-start(f32[2048,128]{1,0:T(8,128)} %get-tuple-element.5) | copy-start | bytes 3145732

commit v2 on v1

--- a/solution.py
+++ b/solution.py
@@ -8,16 +8,17 @@
 from jax.sharding import PartitionSpec as P
 
 RB = 8
+CORES = 2
 MESH = pl.DeviceIdType.MESH
 HIGHEST = lax.Precision.HIGHEST
 
 
 def kernel(
     line, group, lows, cols,
-    a_ref, m_ref, c_out, u_out,
-    a_full, b_buf, c_buf, u_part, u_recv,
+    a_ref, f_ref, structure_ref, panel_ref, u_out,
+    x_buf, mask_buf, m_ref, c_out, a_full, b_buf, c_buf, u_part, u_recv,
     local_sem, a_send, a_recv, b_send, b_recv, z_send,
-    c_send, c_recv, r_send, r_recv, l_send, u_send, u_recv_sem,
+    c_send, c_recv, r_send, r_recv, l_send, u_send, n_send, u_recv_sem,
 ):
     row, col = lax.axis_index("row"), lax.axis_index("col")
     h, p = row // lows, (row % lows) * cols + col
@@ -48,15 +49,41 @@
 
     def each_line(body):
         def step(k, carry):
-            body(k, peer(k, line, h))
+            @pl.when(h >= k)
+            def _():
+                body(h - k)
+
+            @pl.when(h + k < line)
+            def _():
+                body(h + k)
             return carry
         lax.fori_loop(1, line, step, 0)
+
+    places = group // CORES
+
+    def each_chip(body):
+        def step(k, carry):
+            body(k, lax.rem(p + k * CORES, group))
+            return carry
+        lax.fori_loop(1, places, step, 0)
+
+    mate = p + 1 - 2 * lax.rem(p, CORES)
 
     barrier = pltpu.get_barrier_semaphore()
     each_plane(lambda k, q: pl.semaphore_signal(
         barrier, inc=1, device_id=dev(h, q), device_id_type=MESH))
-    each_line(lambda k, hq: pl.semaphore_signal(
+    each_line(lambda hq: pl.semaphore_signal(
         barrier, inc=1, device_id=dev(hq, p), device_id_type=MESH))
+
+    first_block = me * rows // RB
+    for b in range(rows // RB):
+        hit = jnp.where(structure_ref[...] == first_block + b, 1.0, 0.0)
+        mask = jnp.broadcast_to(jnp.max(hit, axis=1, keepdims=True), mask_buf.shape[1:])
+        mask_buf[b] = mask
+        x_buf[b * RB:(b + 1) * RB] = f_ref[b * RB:(b + 1) * RB] * mask[None]
+    for q in range(group):
+        for s in range(per):
+            m_ref[q, :, s * sib_width:(s + 1) * sib_width] = x_buf[:, q * per + s, :]
     pl.semaphore_wait(barrier, group + line - 2)
 
     def piece(hs, q):
@@ -181,19 +208,19 @@
             precision=HIGHEST, preferred_element_type=jnp.float32,
         )
 
-    def r_copy(k, hq):
+    def r_copy(hq):
         return remote(u_part.at[pl.ds(pl.multiple_of(hq * chunk, chunk), chunk)],
-                      u_recv.at[h], r_send.at[k], r_recv.at[h], dev(hq, p))
+                      u_recv.at[h], r_send.at[hq], r_recv.at[h], dev(hq, p))
 
     def c_copy(k, q):
         return remote(c_buf.at[pl.ds(pl.multiple_of(q * rows, rows), rows)], c_out.at[p],
                       c_send.at[k], c_recv.at[p], dev(h, q))
 
-    each_line(lambda k, hq: r_copy(k, hq).start())
+    each_line(lambda hq: r_copy(hq).start())
     each_plane(lambda k, q: c_copy(k, q).start())
     c_out[p] = c_buf[pl.ds(pl.multiple_of(p * rows, rows), rows), :]
     u_recv[h] = u_part[pl.ds(pl.multiple_of(h * chunk, chunk), chunk), :]
-    each_line(lambda k, hq: remote(
+    each_line(lambda hq: remote(
         u_recv.at[hq], u_recv.at[hq], r_send.at[0], r_recv.at[hq], dev(h, p)).wait_recv())
     total = u_recv[0]
     for hs in range(1, line):
@@ -204,32 +231,58 @@
 
     u_out[u_at(h, p), :] = total
 
-    def l_copy(k, hq):
+    def l_copy(hq):
         here = u_out.at[u_at(h, p)]
-        return remote(here, here, l_send.at[k], u_recv_sem.at[me], dev(hq, p))
+        return remote(here, here, l_send.at[hq], u_recv_sem.at[me], dev(hq, p))
 
     def u_copy(hs, k, q):
         here = u_out.at[u_at(hs, p)]
         return remote(here, here, u_send.at[hs, k], u_recv_sem.at[hs * group + p], dev(h, q))
 
+    def n_copy(hs, k, q):
+        here = u_out.at[u_at(hs, q)]
+        return remote(here, here, n_send.at[hs, k], u_recv_sem.at[hs * group + q], dev(h, mate))
+
     def u_wait(hs, q):
         here = u_out.at[u_at(hs, q)]
         remote(here, here, l_send.at[0], u_recv_sem.at[hs * group + q], dev(h, p)).wait_recv()
 
-    each_line(lambda k, hq: l_copy(k, hq).start())
-    each_plane(lambda k, q: u_copy(h, k, q).start())
-
-    def spread(k, hq):
+    each_line(lambda hq: l_copy(hq).start())
+
+    def spread(hs):
+        each_chip(lambda k, q: u_copy(hs, k, q).start())
+        n_copy(hs, 0, p).start()
+
+    spread(h)
+
+    def pass_on(hq):
         u_wait(hq, p)
-        each_plane(lambda j, q: u_copy(hq, j, q).start())
-
-    each_line(spread)
+        spread(hq)
+
+    each_line(pass_on)
+
+    each_plane(lambda k, q: remote(
+        c_out.at[q], c_out.at[q], c_send.at[0], c_recv.at[q], dev(h, p)).wait_recv())
+    for q in range(group):
+        for s in range(per):
+            x_buf[:, q * per + s, :] = c_out[q, :, s * sib_width:(s + 1) * sib_width]
+    for b in range(rows // RB):
+        panel_ref[b * RB:(b + 1) * RB] = -x_buf[b * RB:(b + 1) * RB] * mask_buf[b][None]
+
+    def hand_over(hs):
+        def one(k, q):
+            u_wait(hs, q)
+            n_copy(hs, k, q).start()
+        each_chip(one)
+
+    hand_over(h)
+    each_line(hand_over)
 
     each_plane(lambda k, q: b_copy(k, q).wait_send())
     each_plane(lambda k, q: a_copy(k, q).wait_send())
     each_plane(lambda k, q: c_copy(k, q).wait_send())
-    each_line(lambda k, hq: r_copy(k, hq).wait_send())
-    each_line(lambda k, hq: l_copy(k, hq).wait_send())
+    each_line(lambda hq: r_copy(hq).wait_send())
+    each_line(lambda hq: l_copy(hq).wait_send())
 
     def drain(hs, carry):
         whole = b_buf.at[pl.ds(pl.multiple_of(hs * slab, slab), slab)]
@@ -242,13 +295,14 @@
         def _():
             remote(whole, whole, z_send.at[1, hs], b_recv.at[0], dev(h, p)).wait_send()
 
-        each_plane(lambda k, q: u_copy(hs, k, q).wait_send())
-        each_plane(lambda k, q: u_wait(hs, q))
+        n_copy(hs, 0, p).wait_send()
+        each_chip(lambda k, q: u_copy(hs, k, q).wait_send())
+        each_chip(lambda k, q: n_copy(hs, k, q).wait_send())
+        u_wait(hs, mate)
+        each_chip(lambda k, q: u_wait(hs, q + mate - p))
         return carry
 
     lax.fori_loop(0, line, drain, 0)
-    each_plane(lambda k, q: remote(
-        c_out.at[q], c_out.at[q], c_send.at[0], c_recv.at[q], dev(h, p)).wait_recv())
 
 
 def per_device(row_devices, col_devices, ancestor, factor, diag_inv, structure):
@@ -257,24 +311,22 @@
     line, group = row_devices // lows, lows * col_devices
     per = count_sib // group
     chunk = per * width // line
-    first_row = (lax.axis_index("row") * col_devices + lax.axis_index("col")) * local_rows
-    block_ids = (first_row + jnp.arange(local_rows, dtype=jnp.int32)) // RB
-    matches = block_ids[:, None, None] == structure[None, :, :]
-    row_mask = jnp.any(matches, axis=2).astype(jnp.float32)
-    masked = factor * row_mask[:, :, None]
-    sent = jnp.transpose(masked.reshape(local_rows, group, per * width), (1, 0, 2))
     dma = pltpu.SemaphoreType.DMA
     vmem = pl.BlockSpec(memory_space=pltpu.VMEM)
     f32 = jnp.float32
-    product, update = pl.pallas_call(
+    panel, update = pl.pallas_call(
         functools.partial(kernel, line, group, lows, col_devices),
         out_shape=(
-            jax.ShapeDtypeStruct((group, local_rows, per * width), f32),
+            jax.ShapeDtypeStruct(factor.shape, f32),
             jax.ShapeDtypeStruct((count_sib * width, width), f32),
         ),
-        in_specs=[vmem, vmem],
+        in_specs=[vmem, vmem, vmem],
         out_specs=(vmem, vmem),
         scratch_shapes=[
+            pltpu.VMEM(factor.shape, f32),
+            pltpu.VMEM((local_rows // RB, count_sib, width), f32),
+            pltpu.VMEM((group, local_rows, per * width), f32),
+            pltpu.VMEM((group, local_rows, per * width), f32),
             pltpu.VMEM((group,) + ancestor.shape, f32),
             pltpu.VMEM((line * group * local_rows, per * width), f32),
             pltpu.VMEM((group * local_rows, per * width), f32),
@@ -282,12 +334,10 @@
             pltpu.VMEM((line, chunk, width), f32),
             dma((2,)), dma((group,)), dma((group,)), dma((group,)), dma((line * group,)),
             dma((2, line)), dma((group,)), dma((group,)), dma((line,)), dma((line,)),
-            dma((line,)), dma((line, group)), dma((line * group,)),
+            dma((line,)), dma((line, group // CORES)), dma((line, group // CORES)), dma((line * group,)),
         ],
         compiler_params=pltpu.CompilerParams(collective_id=0, has_side_effects=True),
-    )(ancestor, sent)
-    product = jnp.transpose(product, (1, 0, 2)).reshape(local_rows, count_sib, width)
-    panel = -product * row_mask[:, :, None]
+    )(ancestor, factor, structure)
     return panel, diag_inv + update.reshape(count_sib, width, width)
 
 

time: 54.3 us -> 48.2 us (0.89)
  Pallas kernels: 46.8 us -> 44 us
  other arithmetic: 4.83 us -> 2.69 us
  local copies, waits for them, and re-layouts: 1.72 us -> 0.71 us
    pallas_call x1, Pallas kernels: 46.8 us -> 44 us  [per_device(): pl.pallas_call(functools.partial(kernel, line, group, lows, col_devices),...]
    mul x2 -> x0, other arithmetic: 1.92 us -> none  [the longest x1 1.08 us: per_device(): masked = factor * row_mask[:, :, None]]
    add x1, other arithmetic: 1.08 us -> 2.69 us  [per_device(): return (panel, diag_inv + update.reshape(count_sib, width, width))]
    neg x1 -> x0, other arithmetic: 1.12 us -> none  [per_device(): panel = -product * row_mask[:, :, None]]
    reshape x2 -> x0, local copies, waits for them, and re-layouts: 0.86 us -> none  [per_device(): masked.reshape(local_rows, group, per * width)]
    reduce_or x1 -> x0, other arithmetic: 0.69 us -> none  [per_device(): row_mask = jnp.any(matches, axis=2).astype(jnp.float32)]
where the time goes in v2:
time: 48.2 us; the launch traced here: 48.1 us
  Pallas kernels  44 us (91%)
  other arithmetic  2.69 us (6%)
  local copies, waits for them, and re-layouts  0.71 us (1%)
  between operations  0.65 us (1%)
    pallas_call x1, Pallas kernels, per_device(): pl.pallas_call(functools.partial(kernel, line, group, lows, col_devices),...  44 us
    add x1, other arithmetic, per_device(): return (panel, diag_inv + update.reshape(count_sib, width, width))  2.69 us

profile of v2, /device:TPU:0, one launch (start us, length us, event | category | flops | bytes accessed | tf_op | source)
XLA Modules:
  0.0 48.1 jit_solution(2448510709418017797)
XLA Ops:
  0.6 44.0 %shard_map.59 = (f32[32,16,128]{2,1,0:T(8,128)}, f32[2048,128]{1,0:T(8,128)}) custom-call(f32[128,256]{1,0:T(8,128)} %a_ref.1, f32[32,16,128]{2,1,0:T(8,128)} %f_ref.1, s32[16,96]{1,0:T(8,128)} %structure_ref.1), custom_call_target="tpu_custom_call" | custom-call | tf_op jit(solution)/shard_map/pallas_call | solution.py:317
  44.7 0.0 copy-start
  44.7 2.7 %add.3 = f32[16,128,128]{2,1,0:T(8,128)} add(f32[16,128,128]{2,1,0:T(8,128)} %param.6, f32[16,128,128]{2,1,0:T(8,128)} %bitcast.1) | non-fusion elementwise | flops 262144 | bytes 3145728 | tf_op jit(solution)/shard_map/add | solution.py:341
  47.4 0.0 copy-done
  47.4 0.7 %copy.7 = f32[32,16,128]{2,1,0:T(8,128)} copy(f32[32,16,128]{2,1,0:T(8,128)S(1)} %copy-done) | data formatting | bytes 524288
Async XLA Ops:
  44.7 2.7 %copy-start = (f32[32,16,128]{2,1,0:T(8,128)S(1)}, f32[32,16,128]{2,1,0:T(8,128)}, u32[]{:S(2)}) copy-start(f32[32,16,128]{2,1,0:T(8,128)} %get-tuple-element.8) | copy-start | bytes 786436

commit v3 on v2

--- a/solution.py
+++ b/solution.py
@@ -15,8 +15,8 @@
 
 def kernel(
     line, group, lows, cols,
-    a_ref, f_ref, structure_ref, panel_ref, u_out,
-    x_buf, mask_buf, m_ref, c_out, a_full, b_buf, c_buf, u_part, u_recv,
+    a_ref, f_ref, structure_ref, diag_ref, panel_ref, u_out,
+    d_buf, x_buf, mask_buf, m_ref, c_out, a_full, b_buf, c_buf, u_part, u_recv,
     local_sem, a_send, a_recv, b_send, b_recv, z_send,
     c_send, c_recv, r_send, r_recv, l_send, u_send, n_send, u_recv_sem,
 ):
@@ -69,6 +69,11 @@
 
     mate = p + 1 - 2 * lax.rem(p, CORES)
 
+    def u_at(hs, q):
+        return pl.ds(pl.multiple_of((q * line + hs) * chunk, chunk), chunk)
+
+    own_diag = pltpu.make_async_copy(diag_ref.at[u_at(h, p)], d_buf, local_sem.at[2])
+    own_diag.start()
     barrier = pltpu.get_barrier_semaphore()
     each_plane(lambda k, q: pl.semaphore_signal(
         barrier, inc=1, device_id=dev(h, q), device_id_type=MESH))
@@ -226,10 +231,8 @@
     for hs in range(1, line):
         total = total + u_recv[hs]
 
-    def u_at(hs, q):
-        return pl.ds(pl.multiple_of((q * line + hs) * chunk, chunk), chunk)
-
-    u_out[u_at(h, p), :] = total
+    own_diag.wait()
+    u_out[u_at(h, p), :] = d_buf[...] + total
 
     def l_copy(hq):
         here = u_out.at[u_at(h, p)]
@@ -317,12 +320,13 @@
     panel, update = pl.pallas_call(
         functools.partial(kernel, line, group, lows, col_devices),
         out_shape=(
-            jax.ShapeDtypeStruct(factor.shape, f32),
-            jax.ShapeDtypeStruct((count_sib * width, width), f32),
+            pltpu.VMEM(factor.shape, f32),
+            pltpu.VMEM((count_sib * width, width), f32),
         ),
-        in_specs=[vmem, vmem, vmem],
+        in_specs=[vmem, vmem, vmem, pl.BlockSpec(memory_space=pl.ANY)],
         out_specs=(vmem, vmem),
         scratch_shapes=[
+            pltpu.VMEM((chunk, width), f32),
             pltpu.VMEM(factor.shape, f32),
             pltpu.VMEM((local_rows // RB, count_sib, width), f32),
             pltpu.VMEM((group, local_rows, per * width), f32),
@@ -332,13 +336,13 @@
             pltpu.VMEM((group * local_rows, per * width), f32),
             pltpu.VMEM((per * width, width), f32),
             pltpu.VMEM((line, chunk, width), f32),
-            dma((2,)), dma((group,)), dma((group,)), dma((group,)), dma((line * group,)),
+            dma((3,)), dma((group,)), dma((group,)), dma((group,)), dma((line * group,)),
             dma((2, line)), dma((group,)), dma((group,)), dma((line,)), dma((line,)),
             dma((line,)), dma((line, group // CORES)), dma((line, group // CORES)), dma((line * group,)),
         ],
         compiler_params=pltpu.CompilerParams(collective_id=0, has_side_effects=True),
-    )(ancestor, factor, structure)
-    return panel, diag_inv + update.reshape(count_sib, width, width)
+    )(ancestor, factor, structure, diag_inv.reshape(count_sib * width, width))
+    return panel, update.reshape(count_sib, width, width)
 
 
 def solution(mesh):

time: 48.2 us -> 45.5 us (0.944)
  other arithmetic: 2.69 us -> 0 us
  Pallas kernels: 44 us -> 43 us
  local copies, waits for them, and re-layouts: 0.71 us -> 1.67 us
    add x1 -> x0, other arithmetic: 2.69 us -> none  [per_device(): return (panel, diag_inv + update.reshape(count_sib, width, width))]
    pallas_call x1, Pallas kernels: 44 us -> 43 us  [per_device(): pl.pallas_call(functools.partial(kernel, line, group, lows, col_devices),...]
    unnamed x3 -> x2, local copies, waits for them, and re-layouts: 0.71 us -> 1.67 us
where the time goes in v3:
time: 45.5 us; the launch traced here: 45.3 us
  Pallas kernels  43 us (95%)
  local copies, waits for them, and re-layouts  1.67 us (4%)
  between operations  0.64 us (1%)
    pallas_call x1, Pallas kernels, per_device(): pl.pallas_call(functools.partial(kernel, line, group, lows, col_devices),...  43 us
    unnamed x2, local copies, waits for them, and re-layouts  1.67 us

profile of v3, /device:TPU:0, one launch (start us, length us, event | category | flops | bytes accessed | tf_op | source)
XLA Modules:
  0.0 45.3 jit_solution(6808139096048621042)
XLA Ops:
  0.6 43.0 %shard_map.59 = (f32[32,16,128]{2,1,0:T(8,128)S(1)}, f32[2048,128]{1,0:T(8,128)S(1)}) custom-call(f32[128,256]{1,0:T(8,128)} %a_ref.1, f32[32,16,128]{2,1,0:T(8,128)} %f_ref.1, s32[16,96]{1,0:T(8,128)} %structure_ref.1, f32[2048,128]{1,0:T(8,128)} %bitcast.3), custom_call_target="tpu_custom_call" | custom-call | tf_op jit(solution)/shard_map/pallas_call | solution.py:320
  43.6 0.7 %copy.8 = f32[32,16,128]{2,1,0:T(8,128)} copy(f32[32,16,128]{2,1,0:T(8,128)S(1)} %get-tuple-element.6) | data formatting | bytes 524288
  44.3 1.0 %copy.9 = f32[16,128,128]{2,1,0:T(8,128)} copy(f32[16,128,128]{2,1,0:T(8,128)S(1)} %bitcast.2) | data formatting | bytes 2097152

commit v4 on v3

--- a/solution.py
+++ b/solution.py
@@ -15,8 +15,8 @@
 
 def kernel(
     line, group, lows, cols,
-    a_ref, f_ref, structure_ref, diag_ref, panel_ref, u_out,
-    d_buf, x_buf, mask_buf, m_ref, c_out, a_full, b_buf, c_buf, u_part, u_recv,
+    a_in, f_in, structure_in, diag_ref, panel_ref, u_out,
+    f_ref, structure_ref, d_buf, x_buf, mask_buf, m_ref, c_out, a_full, b_buf, c_buf, u_part, u_recv,
     local_sem, a_send, a_recv, b_send, b_recv, z_send,
     c_send, c_recv, r_send, r_recv, l_send, u_send, n_send, u_recv_sem,
 ):
@@ -74,12 +74,20 @@
 
     own_diag = pltpu.make_async_copy(diag_ref.at[u_at(h, p)], d_buf, local_sem.at[2])
     own_diag.start()
+    own_f = pltpu.make_async_copy(f_in, f_ref, local_sem.at[3])
+    own_f.start()
+    own_structure = pltpu.make_async_copy(structure_in, structure_ref, local_sem.at[4])
+    own_structure.start()
+    own_a = pltpu.make_async_copy(a_in, a_full.at[p], local_sem.at[0])
+    own_a.start()
     barrier = pltpu.get_barrier_semaphore()
     each_plane(lambda k, q: pl.semaphore_signal(
         barrier, inc=1, device_id=dev(h, q), device_id_type=MESH))
     each_line(lambda hq: pl.semaphore_signal(
         barrier, inc=1, device_id=dev(hq, p), device_id_type=MESH))
 
+    own_structure.wait()
+    own_f.wait()
     first_block = me * rows // RB
     for b in range(rows // RB):
         hit = jnp.where(structure_ref[...] == first_block + b, 1.0, 0.0)
@@ -108,13 +116,12 @@
                b_recv.at[hs * group + q], target).start()
 
     def a_copy(k, q):
-        return remote(a_ref, a_full.at[p], a_send.at[k], a_recv.at[p], dev(h, q))
-
-    own_a = pltpu.make_async_copy(a_ref, a_full.at[p], local_sem.at[0])
+        return remote(a_full.at[p], a_full.at[p], a_send.at[k], a_recv.at[p], dev(h, q))
+
     own_b = pltpu.make_async_copy(m_ref.at[p], piece(h, p), local_sem.at[1])
     own_b.start()
     each_plane(lambda k, q: b_copy(k, q).start())
-    own_a.start()
+    own_a.wait()
     own_b.wait()
 
     def first(k, carry):
@@ -165,10 +172,9 @@
     lax.fori_loop(1, line - 1, relay, 0)
 
     c_buf[...] = jnp.zeros_like(c_buf)
-    own_a.wait()
     each_plane(lambda k, q: remote(
         a_full.at[q], a_full.at[q], a_send.at[0], a_recv.at[q], dev(h, p)).wait_recv())
-    a_rows, depth = a_ref.shape
+    a_rows, depth = a_in.shape
     step = min(slab, depth)
 
     def multiply(hs):
@@ -308,6 +314,15 @@
     lax.fori_loop(0, line, drain, 0)
 
 
+def leave(panel_in, update_in, panel_out, update_out, sem):
+    first = pltpu.make_async_copy(update_in, update_out, sem.at[0])
+    second = pltpu.make_async_copy(panel_in, panel_out, sem.at[1])
+    first.start()
+    second.start()
+    first.wait()
+    second.wait()
+
+
 def per_device(row_devices, col_devices, ancestor, factor, diag_inv, structure):
     local_rows, count_sib, width = factor.shape
     lows = max(1, min(row_devices, count_sib // (2 * col_devices)))
@@ -316,6 +331,7 @@
     chunk = per * width // line
     dma = pltpu.SemaphoreType.DMA
     vmem = pl.BlockSpec(memory_space=pltpu.VMEM)
+    anywhere = pl.BlockSpec(memory_space=pl.ANY)
     f32 = jnp.float32
     panel, update = pl.pallas_call(
         functools.partial(kernel, line, group, lows, col_devices),
@@ -323,9 +339,11 @@
             pltpu.VMEM(factor.shape, f32),
             pltpu.VMEM((count_sib * width, width), f32),
         ),
-        in_specs=[vmem, vmem, vmem, pl.BlockSpec(memory_space=pl.ANY)],
+        in_specs=[anywhere] * 4,
         out_specs=(vmem, vmem),
         scratch_shapes=[
+            pltpu.VMEM(factor.shape, f32),
+            pltpu.VMEM(structure.shape, structure.dtype),
             pltpu.VMEM((chunk, width), f32),
             pltpu.VMEM(factor.shape, f32),
             pltpu.VMEM((local_rows // RB, count_sib, width), f32),
@@ -336,12 +354,21 @@
             pltpu.VMEM((group * local_rows, per * width), f32),
             pltpu.VMEM((per * width, width), f32),
             pltpu.VMEM((line, chunk, width), f32),
-            dma((3,)), dma((group,)), dma((group,)), dma((group,)), dma((line * group,)),
+            dma((5,)), dma((group,)), dma((group,)), dma((group,)), dma((line * group,)),
             dma((2, line)), dma((group,)), dma((group,)), dma((line,)), dma((line,)),
             dma((line,)), dma((line, group // CORES)), dma((line, group // CORES)), dma((line * group,)),
         ],
         compiler_params=pltpu.CompilerParams(collective_id=0, has_side_effects=True),
     )(ancestor, factor, structure, diag_inv.reshape(count_sib * width, width))
+    panel, update = pl.pallas_call(
+        leave,
+        out_shape=(
+            jax.ShapeDtypeStruct(panel.shape, f32), jax.ShapeDtypeStruct(update.shape, f32),
+        ),
+        in_specs=[vmem] * 2,
+        out_specs=(anywhere, anywhere),
+        scratch_shapes=[dma((2,))],
+    )(pltpu.with_memory_space_constraint(panel, pltpu.VMEM), pltpu.with_memory_space_constraint(update, pltpu.VMEM))
     return panel, update.reshape(count_sib, width, width)
 
 

time: 45.5 us -> 43.9 us (0.965)
  local copies, waits for them, and re-layouts: 1.67 us -> 0 us
    unnamed x2 -> x0, local copies, waits for them, and re-layouts: 1.67 us -> none
    pallas_call x0 -> x1, Pallas kernels: none -> 1.07 us  [per_device(): pl.pallas_call(leave, out_shape=(jax.ShapeDtypeStruct(panel.shape, f32),...]
    pallas_call x1, Pallas kernels: 43 us -> 42.1 us  [per_device(): pl.pallas_call(functools.partial(kernel, line, group, lows, col_devices),...]
where the time goes in v4:
time: 43.9 us; the launch traced here: 43.8 us
  Pallas kernels  43.1 us (98%)
  between operations  0.64 us (1%)
    pallas_call x1, Pallas kernels, per_device(): pl.pallas_call(functools.partial(kernel, line, group, lows, col_devices),...  42.1 us
    pallas_call x1, Pallas kernels, per_device(): pl.pallas_call(leave, out_shape=(jax.ShapeDtypeStruct(panel.shape, f32),...  1.07 us

profile of v4, /device:TPU:0, one launch (start us, length us, event | category | flops | bytes accessed | tf_op | source)
XLA Modules:
  0.0 43.8 jit_solution(7909932476541938983)
XLA Ops:
  0.6 42.1 %shard_map.59 = (f32[32,16,128]{2,1,0:T(8,128)S(1)}, f32[2048,128]{1,0:T(8,128)S(1)}) custom-call(f32[128,256]{1,0:T(8,128)} %a_in.1, f32[32,16,128]{2,1,0:T(8,128)} %f_in.1, s32[16,96]{1,0:T(8,128)} %structure_in.1, f32[2048,128]{1,0:T(8,128)} %bitcast.2), custom_call_target="tpu_custom_call" | custom-call | tf_op jit(solution)/shard_map/pallas_call | solution.py:336
  42.7 1.1 %shard_map.60 = (f32[32,16,128]{2,1,0:T(8,128)}, f32[2048,128]{1,0:T(8,128)}) custom-call(f32[32,16,128]{2,1,0:T(8,128)S(1)} %get-tuple-element.6.panel_in, f32[2048,128]{1,0:T(8,128)S(1)} %get-tuple-element.7.update_in), custom_call_target="tpu_custom_call" | custom-call | tf_op jit(solution)/shard_map/pallas_call | solution.py:363

commit v5 on v4

--- a/solution.py
+++ b/solution.py
@@ -139,12 +139,10 @@
         def _():
             forward(h, q, False)
 
-        @pl.when(k == 0)
-        def _():
-            each_plane(lambda j, r: a_copy(j, r).start())
         return carry
 
     lax.fori_loop(0, group, first, 0)
+    each_plane(lambda k, q: a_copy(k, q).start())
 
     def relay(t, carry):
         def one(k, inner):

time: 43.9 us -> 43.5 us (level)
    pallas_call x1, Pallas kernels: 42.1 us -> 41.6 us  [per_device(): pl.pallas_call(functools.partial(kernel, line, group, lows, col_devices),...]
where the time goes in v5:
time: 43.5 us; the launch traced here: 43.3 us
  Pallas kernels  42.7 us (98%)
  between operations  0.64 us (1%)
    pallas_call x1, Pallas kernels, per_device(): pl.pallas_call(functools.partial(kernel, line, group, lows, col_devices),...  41.6 us
    pallas_call x1, Pallas kernels, per_device(): pl.pallas_call(leave, out_shape=(jax.ShapeDtypeStruct(panel.shape, f32),...  1.07 us

profile of v5, /device:TPU:0, one launch (start us, length us, event | category | flops | bytes accessed | tf_op | source)
XLA Modules:
  0.0 43.3 jit_solution(6973988034526376709)
XLA Ops:
  0.6 41.6 %shard_map.59 = (f32[32,16,128]{2,1,0:T(8,128)S(1)}, f32[2048,128]{1,0:T(8,128)S(1)}) custom-call(f32[128,256]{1,0:T(8,128)} %a_in.1, f32[32,16,128]{2,1,0:T(8,128)} %f_in.1, s32[16,96]{1,0:T(8,128)} %structure_in.1, f32[2048,128]{1,0:T(8,128)} %bitcast.2), custom_call_target="tpu_custom_call" | custom-call | tf_op jit(solution)/shard_map/pallas_call | solution.py:334
  42.2 1.1 %shard_map.60 = (f32[32,16,128]{2,1,0:T(8,128)}, f32[2048,128]{1,0:T(8,128)}) custom-call(f32[32,16,128]{2,1,0:T(8,128)S(1)} %get-tuple-element.6.panel_in, f32[2048,128]{1,0:T(8,128)S(1)} %get-tuple-element.7.update_in), custom_call_target="tpu_custom_call" | custom-call | tf_op jit(solution)/shard_map/pallas_call | solution.py:361
